TPU v7x, 256 devices: a whole 4x4x8 slice. The times are simulated.
256 devices in a mesh: tile: 32 (over z_hi, x, core), energy: 8 (over z_lo, y).
Axes of the slice: x: 4, y: 4, z: 8 (z_hi: 4, z_lo: 2; z = z_hi * 2 + z_lo), core: 2. Of those that a mesh axis runs over, the one named last changes fastest.
Arguments:
- object_tiles: float32 [8, 2, 8192, 256], P('energy', None, 'tile'), may hold values from -4 to 4
- probe_field: float32 [8, 2, 128, 128], P('energy'), may hold values from -4 to 4
- intensity: bfloat16 [8, 32, 8, 128, 128], P('energy', 'tile'), may hold values from 0.019897461 to 2
- row_offsets: int32 [32, 8], P('tile'), may hold values from -64 to 192, as said below
- col_offsets: int32 [32, 8], P('tile'), may hold values from 0 to 128
- tile_counts: int32 [32], P('tile'), may hold values from 3 to 8
- material_spectra: float32 [8, 3], replicated, may hold values from 0.2 to 2
Outputs:
- material_maps: float32 [3, 8192, 256], P(None, 'tile')
- model_object: float32 [8, 2, 8192, 256], P('energy', None, 'tile')
Inputs may be any that keep to these rules, and one draw needn't show every extreme that they name: `row_offsets`: in every tile one of slots 0 and 1 starts at -64 and the other at 192.
All inputs are finite; a program needn't handle non-finite values.
Results may differ from a plain program's by a relative error of at most 0.0003.
Values sent between devices are 32-bit elements; how exact they have to be, the bound alone decides.
A program may use at most 64 MiB of HBM per device.

v0:
```python
import math
import jax
import jax.numpy as jnp
from jax import lax
from jax.sharding import PartitionSpec as P

PROBE = 128
NN_ITERS = 8
SMOOTH = 0.01
DAMPING = 0.5


def with_halo(x, sides, width):
    for axis, dim in sides:
        count, length = (lax.axis_size(axis), x.shape[dim])
        up = [(i, (i + 1) % count) for i in range(count - 1)]
        down = [(j, i) for i, j in up]
        last = lax.slice_in_dim(x, length - width, length, axis=dim)
        initial = lax.slice_in_dim(x, 0, width, axis=dim)
        before = lax.ppermute(last, axis, up)
        after = lax.ppermute(initial, axis, down)
        x = jnp.concatenate([before, x, after], axis=dim)
    return x


def from_behind(value, axis, steps):
    count = lax.axis_size(axis)
    initial, last = (max(0, -steps), min(count, count - steps))
    return lax.ppermute(value, axis, [(source, source + steps) for source in range(initial, last)])


def left_apply(table, stack):
    return jnp.einsum(
        "jk,pkl->pjl",
        table,
        stack,
        precision=lax.Precision.HIGHEST,
        preferred_element_type=jnp.float32,
    )


def right_apply(stack, table):
    return jnp.einsum(
        "pjk,kl->pjl",
        stack,
        table,
        precision=lax.Precision.HIGHEST,
        preferred_element_type=jnp.float32,
    )


def tables(length):
    indices = jnp.arange(length, dtype=jnp.int32)
    angles = (
        2.0 * math.pi / length * (indices[:, None] * indices[None, :] % length).astype(jnp.float32)
    )
    return (jnp.cos(angles) / math.sqrt(length), jnp.sin(angles) / math.sqrt(length))


def transform(real_in, imag_in, cos_table, sin_table, direction):
    signed = direction * sin_table
    half_real = left_apply(cos_table, real_in) + left_apply(signed, imag_in)
    half_imag = left_apply(cos_table, imag_in) - left_apply(signed, real_in)
    out_real = right_apply(half_real, cos_table) + right_apply(half_imag, signed)
    out_imag = right_apply(half_imag, cos_table) - right_apply(half_real, signed)
    return (out_real, out_imag)


def unmix_maps(attenuation, spectra):
    step_size = 1.0 / jnp.sum(spectra * spectra)
    materials = jnp.zeros((spectra.shape[1],) + attenuation.shape[1:], attenuation.dtype)
    for iteration in range(NN_ITERS):
        predicted = jnp.sum(spectra[:, :, None, None] * materials[None], axis=1)
        mismatch = predicted - attenuation
        gradient = jnp.sum(spectra[:, :, None, None] * mismatch[:, None], axis=0)
        materials = jnp.maximum(materials - step_size * gradient, 0.0)
    return materials


def body(
    object_tiles, probe_field, intensity, row_offsets, col_offsets, tile_counts, material_spectra
):
    current = object_tiles[0]
    probe_re = probe_field[0, 0]
    probe_im = probe_field[0, 1]
    samples = intensity[0, 0]
    live_count = tile_counts[0]
    width = PROBE
    depth = PROBE // 2
    side = current.shape[1]
    slots = row_offsets.shape[1]
    cos_table, sin_table = tables(width)
    power = probe_re * probe_re + probe_im * probe_im
    row_starts = row_offsets[0] + depth
    col_starts = col_offsets[0]
    active = (jnp.arange(slots, dtype=jnp.int32) < live_count)[:, None, None]
    roots = jnp.sqrt(samples.astype(jnp.float32))
    extended = with_halo(current, (("tile", 1),), depth)

    def cut_window(row_start, col_start):
        anchor = jnp.zeros((), jnp.int32)
        return lax.dynamic_slice(extended, (anchor, row_start, col_start), (2, width, width))

    windows = jax.vmap(cut_window)(row_starts, col_starts)
    exit_re = probe_re * windows[:, 0] - probe_im * windows[:, 1]
    exit_im = probe_re * windows[:, 1] + probe_im * windows[:, 0]
    spec_re, spec_im = transform(exit_re, exit_im, cos_table, sin_table, 1.0)
    factor = roots / jnp.sqrt(spec_re * spec_re + spec_im * spec_im + SMOOTH)
    back_re, back_im = transform(spec_re * factor, spec_im * factor, cos_table, sin_table, -1.0)
    change_re = back_re - exit_re
    change_im = back_im - exit_im
    parts_re = jnp.where(active, probe_re * change_re + probe_im * change_im, 0.0)
    parts_im = jnp.where(active, probe_re * change_im - probe_im * change_re, 0.0)
    placed_power = jnp.where(active, power[None], 0.0)

    def place(position, totals):
        numerator, weights = totals
        row_start = row_starts[position]
        col_start = col_starts[position]
        anchor = jnp.zeros((), jnp.int32)
        parts = jnp.stack([parts_re[position], parts_im[position]])
        previous = lax.dynamic_slice(numerator, (anchor, row_start, col_start), (2, width, width))
        numerator = lax.dynamic_update_slice(
            numerator, previous + parts, (anchor, row_start, col_start)
        )
        older = lax.dynamic_slice(weights, (row_start, col_start), (width, width))
        weights = lax.dynamic_update_slice(
            weights, older + placed_power[position], (row_start, col_start)
        )
        return (numerator, weights)

    init = (jnp.zeros_like(extended), jnp.zeros_like(extended[0]))
    numerator, weights = lax.fori_loop(0, slots, place, init)
    from_above = from_behind((numerator[:, depth + side :], weights[depth + side :]), "tile", 1)
    from_below = from_behind((numerator[:, :depth], weights[:depth]), "tile", -1)
    core_num = numerator[:, depth : depth + side]
    core_weights = weights[depth : depth + side]
    core_num = core_num.at[:, :depth].add(from_above[0]).at[:, side - depth :].add(from_below[0])
    core_weights = core_weights.at[:depth].add(from_above[1]).at[side - depth :].add(from_below[1])
    current = current + core_num / (core_weights + DAMPING)
    squared = current[0] ** 2 + current[1] ** 2 + SMOOTH
    attenuation = -0.5 * jnp.log(squared)
    regrouped = lax.all_to_all(attenuation[None], "energy", split_axis=1, concat_axis=0, tiled=True)
    piece_maps = unmix_maps(regrouped, material_spectra)
    materials = lax.all_gather(piece_maps, "energy", axis=1, tiled=True)
    own_row = lax.dynamic_index_in_dim(
        material_spectra, lax.axis_index("energy"), 0, keepdims=False
    )
    thickness = jnp.sum(own_row[:, None, None] * materials, axis=0)
    scale_out = jnp.exp(-thickness) / jnp.sqrt(squared)
    model_object = (current * scale_out[None])[None]
    return (materials, model_object)


def solution(mesh):
    placed = (
        P("energy", None, "tile", None),
        P("energy", None, None, None),
        P("energy", "tile", None, None, None),
        P("tile", None),
        P("tile", None),
        P("tile"),
        P(),
    )
    return jax.shard_map(
        body,
        mesh=mesh,
        in_specs=placed,
        out_specs=(P(None, "tile", None), P("energy", None, "tile", None)),
        check_vma=False,
    )
```

profile of v0, /device:TPU:128, one launch (start us, length us, event | category | flops | bytes accessed | tf_op | source)
XLA Modules:
  0.0 357.7 jit_solution(117914211898438778)
XLA Ops:
  0.6 1.4 copy.128
  2.1 2.1 collective-permute-start
  4.2 7.9 %collective-permute-start.1 = (f32[2,64,256]{2,0,1:T(2,128)S(1)}, f32[2,64,256]{2,0,1:T(2,128)S(1)}, u32[]{:S(2)}, u32[]{:S(2)}) collective-permute-start(f32[2,64,256]{2,0,1:T(2,128)S(1)} %get-tuple-element.251), channel_id=1, source_target_pairs={{8,0},{16,8},{24,16},{32,24},{40,32},{48,40},{56,48},{64,56},{72,6... | collective-permute-start | bytes 393224 | tf_op jit(solution)/shard_map/ppermute | solution.py:21
  12.1 0.6 copy-done.4
  12.7 0.7 copy-done.5
  14.1 1.7 collective-permute-done.1
  16.2 17.3 %while.21 = (s32[]{:T(128)}, f32[2,384,256]{2,0,1:T(2,128)S(1)}, s32[8,3]{0,1:T(4,128)S(1)}, f32[8,2,128,128]{3,2,0,1:T(8,128)S(1)}, s32[]{:T(128)}) while((s32[]{:T(128)}, f32[2,384,256]{2,0,1:T(2,128)S(1)}, s32[8,3]{0,1:T(4,128)S(1)}, f32[8,2,128,128]{3,2,0,1:T(8,128)S(1)}, s32[]{:T(128)}) %tuple.79), condition=%wide.while_cond.4, body=%wide.while_body.4.sunk | while | flops 2 | bytes 524405 | solution.py:102
  16.2 0.6 fusion.171
  16.8 1.5 constant_dynamic-slice_fusion.12
  19.0 1.5 constant_dynamic-slice_fusion.12
  21.2 1.5 constant_dynamic-slice_fusion.12
  22.7 0.6 fusion.171
  23.3 1.5 constant_dynamic-slice_fusion.12
  24.9 0.6 fusion.171
  25.5 1.5 constant_dynamic-slice_fusion.12
  27.7 1.5 constant_dynamic-slice_fusion.12
  29.8 1.5 constant_dynamic-slice_fusion.12
  32.0 1.5 constant_dynamic-slice_fusion.12
  33.6 1.1 fusion.39
  34.7 1.1 fusion.35
  35.9 1.1 fusion.5
  37.0 1.1 fusion.37
  38.1 1.1 fusion.4
  39.3 1.1 fusion.33
  40.4 1.1 convolution_add_fusion.2
  41.6 1.1 convolution_subtract_fusion.2
  42.7 1.4 fusion.31
  44.1 1.6 fusion.27
  45.7 1.4 fusion.3
  47.1 1.4 fusion.2
  48.5 1.1 fusion.25
  49.7 1.1 fusion.29
  50.8 1.2 fusion
  52.0 1.2 subtract_select_fusion
  53.5 232.1 %while.20 = (s32[]{:T(128)}, f32[2,384,256]{2,0,1:T(2,128)S(1)}, f32[384,256]{1,0:T(8,128)S(1)}, s32[8]{0:T(128)S(1)}, s32[8]{0:T(128)S(1)}, /*index=5*/f32[8,12...) while((s32[]{:T(128)}, f32[2,384,256]{2,0,1:T(2,128)S(1)}, ...), condition=%wide.region_3.4_spmd, body=%wide.region_2.3_spmd.sunk | while | flops 81928 | bytes 1769713 | solution.py:133
  58.9 21.6 %dynamic_update_slice.16 = f32[2,384,256]{2,0,1:T(2,128)S(1)} dynamic-update-slice(f32[2,384,256]{2,0,1:T(2,128)S(1)} %get-tuple-element.369, f32[2,128,128]{2,0,1:T(2,128)S(1)} %copy.134, s32[]{:T(128)} %constant.183.clone.1..sunk, s32[]{:T(128)S(6)} %select_n.174, s32[]{:T(128)S(6)} %select_n.175) | dynamic-update-slice | bytes 262148 | tf_op jit(solution)/shard_map/while/body/eval_jaxpr/dynamic_update_slice | solution.py:123
  80.6 2.0 dynamic_update_slice.17
  88.1 21.6 %dynamic_update_slice.16 = f32[2,384,256]{2,0,1:T(2,128)S(1)} dynamic-update-slice(f32[2,384,256]{2,0,1:T(2,128)S(1)} %get-tuple-element.369, f32[2,128,128]{2,0,1:T(2,128)S(1)} %copy.134, s32[]{:T(128)} %constant.183.clone.1..sunk, s32[]{:T(128)S(6)} %select_n.174, s32[]{:T(128)S(6)} %select_n.175) | dynamic-update-slice | bytes 262148 | tf_op jit(solution)/shard_map/while/body/eval_jaxpr/dynamic_update_slice | solution.py:123
  109.8 1.5 dynamic_update_slice.17
  116.8 21.6 %dynamic_update_slice.16 = f32[2,384,256]{2,0,1:T(2,128)S(1)} dynamic-update-slice(f32[2,384,256]{2,0,1:T(2,128)S(1)} %get-tuple-element.369, f32[2,128,128]{2,0,1:T(2,128)S(1)} %copy.134, s32[]{:T(128)} %constant.183.clone.1..sunk, s32[]{:T(128)S(6)} %select_n.174, s32[]{:T(128)S(6)} %select_n.175) | dynamic-update-slice | bytes 262148 | tf_op jit(solution)/shard_map/while/body/eval_jaxpr/dynamic_update_slice | solution.py:123
  138.4 1.8 dynamic_update_slice.17
  145.7 21.6 %dynamic_update_slice.16 = f32[2,384,256]{2,0,1:T(2,128)S(1)} dynamic-update-slice(f32[2,384,256]{2,0,1:T(2,128)S(1)} %get-tuple-element.369, f32[2,128,128]{2,0,1:T(2,128)S(1)} %copy.134, s32[]{:T(128)} %constant.183.clone.1..sunk, s32[]{:T(128)S(6)} %select_n.174, s32[]{:T(128)S(6)} %select_n.175) | dynamic-update-slice | bytes 262148 | tf_op jit(solution)/shard_map/while/body/eval_jaxpr/dynamic_update_slice | solution.py:123
  167.4 2.0 dynamic_update_slice.17
  174.9 21.6 %dynamic_update_slice.16 = f32[2,384,256]{2,0,1:T(2,128)S(1)} dynamic-update-slice(f32[2,384,256]{2,0,1:T(2,128)S(1)} %get-tuple-element.369, f32[2,128,128]{2,0,1:T(2,128)S(1)} %copy.134, s32[]{:T(128)} %constant.183.clone.1..sunk, s32[]{:T(128)S(6)} %select_n.174, s32[]{:T(128)S(6)} %select_n.175) | dynamic-update-slice | bytes 262148 | tf_op jit(solution)/shard_map/while/body/eval_jaxpr/dynamic_update_slice | solution.py:123
  196.6 1.7 dynamic_update_slice.17
  203.8 21.6 %dynamic_update_slice.16 = f32[2,384,256]{2,0,1:T(2,128)S(1)} dynamic-update-slice(f32[2,384,256]{2,0,1:T(2,128)S(1)} %get-tuple-element.369, f32[2,128,128]{2,0,1:T(2,128)S(1)} %copy.134, s32[]{:T(128)} %constant.183.clone.1..sunk, s32[]{:T(128)S(6)} %select_n.174, s32[]{:T(128)S(6)} %select_n.175) | dynamic-update-slice | bytes 262148 | tf_op jit(solution)/shard_map/while/body/eval_jaxpr/dynamic_update_slice | solution.py:123
  225.4 1.9 dynamic_update_slice.17
  232.8 21.6 %dynamic_update_slice.16 = f32[2,384,256]{2,0,1:T(2,128)S(1)} dynamic-update-slice(f32[2,384,256]{2,0,1:T(2,128)S(1)} %get-tuple-element.369, f32[2,128,128]{2,0,1:T(2,128)S(1)} %copy.134, s32[]{:T(128)} %constant.183.clone.1..sunk, s32[]{:T(128)S(6)} %select_n.174, s32[]{:T(128)S(6)} %select_n.175) | dynamic-update-slice | bytes 262148 | tf_op jit(solution)/shard_map/while/body/eval_jaxpr/dynamic_update_slice | solution.py:123
  254.5 2.0 dynamic_update_slice.17
  262.0 21.6 %dynamic_update_slice.16 = f32[2,384,256]{2,0,1:T(2,128)S(1)} dynamic-update-slice(f32[2,384,256]{2,0,1:T(2,128)S(1)} %get-tuple-element.369, f32[2,128,128]{2,0,1:T(2,128)S(1)} %copy.134, s32[]{:T(128)} %constant.183.clone.1..sunk, s32[]{:T(128)S(6)} %select_n.174, s32[]{:T(128)S(6)} %select_n.175) | dynamic-update-slice | bytes 262148 | tf_op jit(solution)/shard_map/while/body/eval_jaxpr/dynamic_update_slice | solution.py:123
  283.7 1.8 dynamic_update_slice.17
  285.6 1.9 collective-permute-start.4
  287.7 7.9 %collective-permute-start.5 = (f32[64,256]{1,0:T(8,128)S(1)}, f32[64,256]{1,0:T(8,128)S(1)}, u32[]{:S(2)}, u32[]{:S(2)}) collective-permute-start(f32[64,256]{1,0:T(8,128)S(1)} %get-tuple-element.252), channel_id=1, source_target_pairs={{8,0},{16,8},{24,16},{32,24},{40,32},{48,40},{56,48},{64,56},{72,6... | collective-permute-start | bytes 196616 | tf_op jit(solution)/shard_map/ppermute | solution.py:29
  295.6 1.9 collective-permute-start.2
  297.5 8.1 %collective-permute-start.3 = (f32[2,64,256]{2,0,1:T(2,128)S(1)}, f32[2,64,256]{2,0,1:T(2,128)S(1)}, u32[]{:S(2)}, u32[]{:S(2)}) collective-permute-start(f32[2,64,256]{2,0,1:T(2,128)S(1)} %get-tuple-element.248), channel_id=1, source_target_pairs={{8,0},{16,8},{24,16},{32,24},{40,32},{48,40},{56,48},{64,56},{72,6... | collective-permute-start | bytes 393224 | tf_op jit(solution)/shard_map/ppermute | solution.py:29
  306.2 3.0 collective-permute-done.3
  309.3 0.6 divide_add_fusion
  310.0 1.3 log_multiply_fusion
  311.3 4.5 %all-to-all-start = ((f32[1,256,256]{2,0,1:T(1,128)}), f32[1,256,256]{2,0,1:T(1,128)S(1)}, u32[]{:S(2)}, u32[]{:S(2)}) async-start(f32[1,256,256]{2,0,1:T(1,128)} %get-tuple-element.238), calls=%async_computation | async-start | bytes 524288 | tf_op jit(solution)/shard_map/all_to_all | solution.py:143
  316.0 0.6 multiply_reduce_fusion.17
  317.3 5.7 %all-to-all-done = f32[1,256,256]{2,0,1:T(1,128)S(1)} async-done(((f32[1,256,256]{2,0,1:T(1,128)}), f32[1,256,256]{2,0,1:T(1,128)S(1)}, u32[]{:S(2)}, u32[]{:S(2)}) %all-to-all-start) | async-done | bytes 262176 | tf_op jit(solution)/shard_map/all_to_all | solution.py:143
  325.5 29.7 %all_gather.3 = f32[3,256,256]{2,1,0:T(8,128)S(1)} all-gather(f32[3,32,256]{2,1,0:T(8,128)S(1)} %subtract_maximum_fusion), channel_id=1, replica_groups=mesh['tile'=32,'energy'=8] {'energy'}, dimensions={1}, use_global_device_ids=true | all-gather | bytes 884736 | tf_op jit(solution)/shard_map/all_gather | solution.py:145
  356.0 0.8 copy.79
  356.8 0.9 copy.160
  (152 shorter events, 21.6 us)
Async XLA Ops:
  2.1 10.0 %copy-start.2 = (f32[1,2,128,128]{3,2,1,0:T(8,128)S(1)}, f32[1,2,128,128]{3,2,1,0:T(8,128)}, u32[]{:S(2)}) copy-start(f32[1,2,128,128]{3,2,1,0:T(8,128)} %param.18) | copy-start | bytes 393220
  2.1 12.0 %collective-permute-start = (f32[2,64,256]{2,0,1:T(2,128)S(1)}, f32[2,64,256]{2,0,1:T(2,128)S(1)}, u32[]{:S(2)}, u32[]{:S(2)}) collective-permute-start(f32[2,64,256]{2,0,1:T(2,128)S(1)} %get-tuple-element.250), channel_id=1, source_target_pairs={{0,8},{8,16},{16,24},{24,32},{32,40},{40,48},{48,56},{56,64},{64,7... | collective-permute-start | bytes 393224 | tf_op jit(solution)/shard_map/ppermute | solution.py:20
  4.2 11.6 %collective-permute-start.1 = (f32[2,64,256]{2,0,1:T(2,128)S(1)}, f32[2,64,256]{2,0,1:T(2,128)S(1)}, u32[]{:S(2)}, u32[]{:S(2)}) collective-permute-start(f32[2,64,256]{2,0,1:T(2,128)S(1)} %get-tuple-element.251), channel_id=1, source_target_pairs={{8,0},{16,8},{24,16},{32,24},{40,32},{48,40},{56,48},{64,56},{72,6... | collective-permute-start | bytes 393224 | tf_op jit(solution)/shard_map/ppermute | solution.py:21
  12.1 0.7 copy-start.4
  12.7 0.7 copy-start.5
  41.6 1.2 copy-start
  285.6 20.1 %collective-permute-start.4 = (f32[64,256]{1,0:T(8,128)S(1)}, f32[64,256]{1,0:T(8,128)S(1)}, u32[]{:S(2)}, u32[]{:S(2)}) collective-permute-start(f32[64,256]{1,0:T(8,128)S(1)} %get-tuple-element.253), channel_id=1, source_target_pairs={{0,8},{8,16},{16,24},{24,32},{32,40},{40,48},{48,56},{56,64},{64,7... | collective-permute-start | bytes 196616 | tf_op jit(solution)/shard_map/ppermute | solution.py:29
  287.7 17.9 %collective-permute-start.5 = (f32[64,256]{1,0:T(8,128)S(1)}, f32[64,256]{1,0:T(8,128)S(1)}, u32[]{:S(2)}, u32[]{:S(2)}) collective-permute-start(f32[64,256]{1,0:T(8,128)S(1)} %get-tuple-element.252), channel_id=1, source_target_pairs={{8,0},{16,8},{24,16},{32,24},{40,32},{48,40},{56,48},{64,56},{72,6... | collective-permute-start | bytes 196616 | tf_op jit(solution)/shard_map/ppermute | solution.py:29
  295.6 10.5 %collective-permute-start.2 = (f32[2,64,256]{2,0,1:T(2,128)S(1)}, f32[2,64,256]{2,0,1:T(2,128)S(1)}, u32[]{:S(2)}, u32[]{:S(2)}) collective-permute-start(f32[2,64,256]{2,0,1:T(2,128)S(1)} %get-tuple-element.249), channel_id=1, source_target_pairs={{0,8},{8,16},{16,24},{24,32},{32,40},{40,48},{48,56},{56,64},{64,7... | collective-permute-start | bytes 393224 | tf_op jit(solution)/shard_map/ppermute | solution.py:29
  297.5 11.7 %collective-permute-start.3 = (f32[2,64,256]{2,0,1:T(2,128)S(1)}, f32[2,64,256]{2,0,1:T(2,128)S(1)}, u32[]{:S(2)}, u32[]{:S(2)}) collective-permute-start(f32[2,64,256]{2,0,1:T(2,128)S(1)} %get-tuple-element.248), channel_id=1, source_target_pairs={{8,0},{16,8},{24,16},{32,24},{40,32},{48,40},{56,48},{64,56},{72,6... | collective-permute-start | bytes 393224 | tf_op jit(solution)/shard_map/ppermute | solution.py:29
  305.7 3.6 %copy-start.1 = (f32[1,2,256,256]{3,2,1,0:T(8,128)S(1)}, f32[1,2,256,256]{3,2,1,0:T(8,128)}, u32[]{:S(2)}) copy-start(f32[1,2,256,256]{3,2,1,0:T(8,128)} %param.17) | copy-start | bytes 1572868
  309.9 5.8 %copy-start.3 = (f32[8,3]{0,1:T(4,128)S(1)}, f32[8,3]{0,1:T(4,128)}, u32[]{:S(2)}) copy-start(f32[8,3]{0,1:T(4,128)} %param.23) | copy-start | bytes 292
  311.3 11.7 %all-to-all-start = ((f32[1,256,256]{2,0,1:T(1,128)}), f32[1,256,256]{2,0,1:T(1,128)S(1)}, u32[]{:S(2)}, u32[]{:S(2)}) async-start(f32[1,256,256]{2,0,1:T(1,128)} %get-tuple-element.238), calls=%async_computation | async-start | bytes 524288 | tf_op jit(solution)/shard_map/all_to_all | solution.py:143
where the time goes:
time: 359 us; the launch traced here: 358 us
  local copies, waits for them, and re-layouts  222 us (62%)
  starting transfers between devices  34.2 us (10%)
  loops' own time  31.8 us (9%)
  blocking collectives  29.7 us (8%)
  matrix products  19.5 us (5%)
  waiting for transfers between devices  10.8 us (3%)
  other arithmetic  7.17 us (2%)
    dynamic_update_slice x16, local copies, waits for them, and re-layouts, place(): lax.dynamic_update_slice(numerator, previous + parts, (anchor, row_start,...  173 us
    another operation x1, loops' own time, body(): numerator, weights = lax.fori_loop(0, slots, place, init)  31.6 us
    all_gather x1, blocking collectives, body(): materials = lax.all_gather(piece_maps, 'energy', axis=1, tiled=True)  29.7 us
    ppermute x4, starting transfers between devices, from_behind(): lax.ppermute(value, axis, [(source, source + steps) for source in range(i...  19.8 us
    gather x32, local copies, waits for them, and re-layouts  17.1 us
    dynamic_update_slice x8, local copies, waits for them, and re-layouts, place(): lax.dynamic_update_slice(weights, older + placed_power[position], (row_st...  14.9 us
    dot_general x8, matrix products, left_apply(): jnp.einsum('jk,pkl->pjl', table, stack, precision=lax.Precision.HIGHEST,...  10.3 us
    dot_general x8, matrix products, right_apply(): jnp.einsum('pjk,kl->pjl', stack, table, precision=lax.Precision.HIGHEST,...  9.19 us
  transfers between devices with their start and end apart: 7, of which 4 were waited for; matrix products, arithmetic and copies ran while one was open for 0% of the time, Pallas kernels for 0%

commit v1 on v0

--- a/solution.py
+++ b/solution.py
@@ -142,7 +142,8 @@
     attenuation = -0.5 * jnp.log(squared)
     regrouped = lax.all_to_all(attenuation[None], "energy", split_axis=1, concat_axis=0, tiled=True)
     piece_maps = unmix_maps(regrouped, material_spectra)
-    materials = lax.all_gather(piece_maps, "energy", axis=1, tiled=True)
+    stack_2 = jnp.stack([piece_maps] * lax.axis_size("energy"))
+    materials = jnp.concatenate(lax.all_to_all(stack_2, "energy", 0, 0), axis=1)
     own_row = lax.dynamic_index_in_dim(
         material_spectra, lax.axis_index("energy"), 0, keepdims=False
     )

time: 359 us -> 345 us (0.961)
  blocking collectives: 29.7 us -> 0 us
  waiting for transfers between devices: 10.8 us -> 20.2 us
  starting transfers between devices: 34.2 us -> 37.8 us
    all_gather x1 -> x0, blocking collectives: 29.7 us -> none  [body(): materials = lax.all_gather(piece_maps, 'energy', axis=1, tiled=True)]
    all_to_all x0 -> x1, waiting for transfers between devices: none -> 9.22 us  [body(): materials = jnp.concatenate(lax.all_to_all(stack_2, 'energy', 0, 0), axis=1)]
  transfers between devices with their start and end apart: 7 -> 8, of which waited for: 4 -> 5; matrix products, arithmetic and copies ran while one was open for 0% -> 0% of each run, Pallas kernels for 0% -> 0%
where the time goes in v1:
time: 345 us; the launch traced here: 342 us
  local copies, waits for them, and re-layouts  223 us (65%)
  starting transfers between devices  37.8 us (11%)
  loops' own time  31.8 us (9%)
  waiting for transfers between devices  20.2 us (6%)
  matrix products  19.5 us (6%)
  other arithmetic  6.93 us (2%)
    dynamic_update_slice x16, local copies, waits for them, and re-layouts, place(): lax.dynamic_update_slice(numerator, previous + parts, (anchor, row_start,...  173 us
    another operation x1, loops' own time, body(): numerator, weights = lax.fori_loop(0, slots, place, init)  31.6 us
    ppermute x4, starting transfers between devices, from_behind(): lax.ppermute(value, axis, [(source, source + steps) for source in range(i...  19.8 us
    gather x32, local copies, waits for them, and re-layouts  17.1 us
    dynamic_update_slice x8, local copies, waits for them, and re-layouts, place(): lax.dynamic_update_slice(weights, older + placed_power[position], (row_st...  14.9 us
    dot_general x8, matrix products, left_apply(): jnp.einsum('jk,pkl->pjl', table, stack, precision=lax.Precision.HIGHEST,...  10.3 us
    all_to_all x1, waiting for transfers between devices, body(): materials = jnp.concatenate(lax.all_to_all(stack_2, 'energy', 0, 0), axis=1)  9.22 us
    dot_general x8, matrix products, right_apply(): jnp.einsum('pjk,kl->pjl', stack, table, precision=lax.Precision.HIGHEST,...  9.19 us
  transfers between devices with their start and end apart: 8, of which 5 were waited for; matrix products, arithmetic and copies ran while one was open for 0% of the time, Pallas kernels for 0%

profile of v1, /device:TPU:128, one launch (start us, length us, event | category | flops | bytes accessed | tf_op | source)
XLA Modules:
  0.0 342.1 jit_solution(1986755218629877186)
XLA Ops:
  0.6 1.4 copy.157
  2.1 2.1 collective-permute-start
  4.2 7.9 %collective-permute-start.1 = (f32[2,64,256]{2,0,1:T(2,128)S(1)}, f32[2,64,256]{2,0,1:T(2,128)S(1)}, u32[]{:S(2)}, u32[]{:S(2)}) collective-permute-start(f32[2,64,256]{2,0,1:T(2,128)S(1)} %get-tuple-element.257), channel_id=1, source_target_pairs={{8,0},{16,8},{24,16},{32,24},{40,32},{48,40},{56,48},{64,56},{72,6... | collective-permute-start | bytes 393224 | tf_op jit(solution)/shard_map/ppermute | solution.py:21
  12.1 0.6 copy-done.4
  12.7 0.7 copy-done.5
  14.1 1.7 collective-permute-done.1
  16.2 17.3 %while.21 = (s32[]{:T(128)}, f32[2,384,256]{2,0,1:T(2,128)S(1)}, s32[8,3]{0,1:T(4,128)S(1)}, f32[8,2,128,128]{3,2,0,1:T(8,128)S(1)}, s32[]{:T(128)}) while((s32[]{:T(128)}, f32[2,384,256]{2,0,1:T(2,128)S(1)}, s32[8,3]{0,1:T(4,128)S(1)}, f32[8,2,128,128]{3,2,0,1:T(8,128)S(1)}, s32[]{:T(128)}) %tuple.81), condition=%wide.while_cond.4, body=%wide.while_body.4.sunk | while | flops 2 | bytes 524405 | solution.py:102
  16.2 0.6 fusion.172
  16.8 1.5 constant_dynamic-slice_fusion.12
  19.0 1.5 constant_dynamic-slice_fusion.12
  21.2 1.5 constant_dynamic-slice_fusion.12
  23.3 1.5 constant_dynamic-slice_fusion.12
  25.5 1.5 constant_dynamic-slice_fusion.12
  27.7 1.5 constant_dynamic-slice_fusion.12
  29.8 1.5 constant_dynamic-slice_fusion.12
  32.0 1.5 constant_dynamic-slice_fusion.12
  33.6 1.1 fusion.40
  34.7 1.1 fusion.36
  35.9 1.1 fusion.5
  37.0 1.1 fusion.38
  38.1 1.1 fusion.4
  39.3 1.1 fusion.34
  40.4 1.1 convolution_add_fusion.2
  41.6 1.1 convolution_subtract_fusion.2
  42.7 1.4 fusion.32
  44.1 1.6 fusion.28
  45.7 1.4 fusion.3
  47.1 1.4 fusion.2
  48.5 1.1 fusion.26
  49.7 1.1 fusion.30
  50.8 1.2 fusion
  52.0 1.2 subtract_select_fusion
  53.5 232.1 %while.20 = (s32[]{:T(128)}, f32[2,384,256]{2,0,1:T(2,128)S(1)}, f32[384,256]{1,0:T(8,128)S(1)}, s32[8]{0:T(128)S(1)}, s32[8]{0:T(128)S(1)}, /*index=5*/f32[8,12...) while((s32[]{:T(128)}, f32[2,384,256]{2,0,1:T(2,128)S(1)}, ...), condition=%wide.region_3.4_spmd, body=%wide.region_2.3_spmd.sunk | while | flops 81928 | bytes 1769713 | solution.py:133
  58.9 21.6 %dynamic_update_slice.16 = f32[2,384,256]{2,0,1:T(2,128)S(1)} dynamic-update-slice(f32[2,384,256]{2,0,1:T(2,128)S(1)} %get-tuple-element.375, f32[2,128,128]{2,0,1:T(2,128)S(1)} %copy.163, s32[]{:T(128)} %constant.183.clone.1..sunk, s32[]{:T(128)S(6)} %select_n.174, s32[]{:T(128)S(6)} %select_n.175) | dynamic-update-slice | bytes 262148 | tf_op jit(solution)/shard_map/while/body/eval_jaxpr/dynamic_update_slice | solution.py:123
  80.6 2.0 dynamic_update_slice.17
  88.1 21.6 %dynamic_update_slice.16 = f32[2,384,256]{2,0,1:T(2,128)S(1)} dynamic-update-slice(f32[2,384,256]{2,0,1:T(2,128)S(1)} %get-tuple-element.375, f32[2,128,128]{2,0,1:T(2,128)S(1)} %copy.163, s32[]{:T(128)} %constant.183.clone.1..sunk, s32[]{:T(128)S(6)} %select_n.174, s32[]{:T(128)S(6)} %select_n.175) | dynamic-update-slice | bytes 262148 | tf_op jit(solution)/shard_map/while/body/eval_jaxpr/dynamic_update_slice | solution.py:123
  109.8 1.5 dynamic_update_slice.17
  116.8 21.6 %dynamic_update_slice.16 = f32[2,384,256]{2,0,1:T(2,128)S(1)} dynamic-update-slice(f32[2,384,256]{2,0,1:T(2,128)S(1)} %get-tuple-element.375, f32[2,128,128]{2,0,1:T(2,128)S(1)} %copy.163, s32[]{:T(128)} %constant.183.clone.1..sunk, s32[]{:T(128)S(6)} %select_n.174, s32[]{:T(128)S(6)} %select_n.175) | dynamic-update-slice | bytes 262148 | tf_op jit(solution)/shard_map/while/body/eval_jaxpr/dynamic_update_slice | solution.py:123
  138.4 1.8 dynamic_update_slice.17
  145.7 21.6 %dynamic_update_slice.16 = f32[2,384,256]{2,0,1:T(2,128)S(1)} dynamic-update-slice(f32[2,384,256]{2,0,1:T(2,128)S(1)} %get-tuple-element.375, f32[2,128,128]{2,0,1:T(2,128)S(1)} %copy.163, s32[]{:T(128)} %constant.183.clone.1..sunk, s32[]{:T(128)S(6)} %select_n.174, s32[]{:T(128)S(6)} %select_n.175) | dynamic-update-slice | bytes 262148 | tf_op jit(solution)/shard_map/while/body/eval_jaxpr/dynamic_update_slice | solution.py:123
  167.4 2.0 dynamic_update_slice.17
  174.9 21.6 %dynamic_update_slice.16 = f32[2,384,256]{2,0,1:T(2,128)S(1)} dynamic-update-slice(f32[2,384,256]{2,0,1:T(2,128)S(1)} %get-tuple-element.375, f32[2,128,128]{2,0,1:T(2,128)S(1)} %copy.163, s32[]{:T(128)} %constant.183.clone.1..sunk, s32[]{:T(128)S(6)} %select_n.174, s32[]{:T(128)S(6)} %select_n.175) | dynamic-update-slice | bytes 262148 | tf_op jit(solution)/shard_map/while/body/eval_jaxpr/dynamic_update_slice | solution.py:123
  196.6 1.7 dynamic_update_slice.17
  203.8 21.6 %dynamic_update_slice.16 = f32[2,384,256]{2,0,1:T(2,128)S(1)} dynamic-update-slice(f32[2,384,256]{2,0,1:T(2,128)S(1)} %get-tuple-element.375, f32[2,128,128]{2,0,1:T(2,128)S(1)} %copy.163, s32[]{:T(128)} %constant.183.clone.1..sunk, s32[]{:T(128)S(6)} %select_n.174, s32[]{:T(128)S(6)} %select_n.175) | dynamic-update-slice | bytes 262148 | tf_op jit(solution)/shard_map/while/body/eval_jaxpr/dynamic_update_slice | solution.py:123
  225.4 1.9 dynamic_update_slice.17
  232.8 21.6 %dynamic_update_slice.16 = f32[2,384,256]{2,0,1:T(2,128)S(1)} dynamic-update-slice(f32[2,384,256]{2,0,1:T(2,128)S(1)} %get-tuple-element.375, f32[2,128,128]{2,0,1:T(2,128)S(1)} %copy.163, s32[]{:T(128)} %constant.183.clone.1..sunk, s32[]{:T(128)S(6)} %select_n.174, s32[]{:T(128)S(6)} %select_n.175) | dynamic-update-slice | bytes 262148 | tf_op jit(solution)/shard_map/while/body/eval_jaxpr/dynamic_update_slice | solution.py:123
  254.5 2.0 dynamic_update_slice.17
  262.0 21.6 %dynamic_update_slice.16 = f32[2,384,256]{2,0,1:T(2,128)S(1)} dynamic-update-slice(f32[2,384,256]{2,0,1:T(2,128)S(1)} %get-tuple-element.375, f32[2,128,128]{2,0,1:T(2,128)S(1)} %copy.163, s32[]{:T(128)} %constant.183.clone.1..sunk, s32[]{:T(128)S(6)} %select_n.174, s32[]{:T(128)S(6)} %select_n.175) | dynamic-update-slice | bytes 262148 | tf_op jit(solution)/shard_map/while/body/eval_jaxpr/dynamic_update_slice | solution.py:123
  283.7 1.8 dynamic_update_slice.17
  285.6 1.9 collective-permute-start.4
  287.7 7.9 %collective-permute-start.5 = (f32[64,256]{1,0:T(8,128)S(1)}, f32[64,256]{1,0:T(8,128)S(1)}, u32[]{:S(2)}, u32[]{:S(2)}) collective-permute-start(f32[64,256]{1,0:T(8,128)S(1)} %get-tuple-element.258), channel_id=1, source_target_pairs={{8,0},{16,8},{24,16},{32,24},{40,32},{48,40},{56,48},{64,56},{72,6... | collective-permute-start | bytes 196616 | tf_op jit(solution)/shard_map/ppermute | solution.py:29
  295.6 1.9 collective-permute-start.2
  297.5 8.1 %collective-permute-start.3 = (f32[2,64,256]{2,0,1:T(2,128)S(1)}, f32[2,64,256]{2,0,1:T(2,128)S(1)}, u32[]{:S(2)}, u32[]{:S(2)}) collective-permute-start(f32[2,64,256]{2,0,1:T(2,128)S(1)} %get-tuple-element.254), channel_id=1, source_target_pairs={{8,0},{16,8},{24,16},{32,24},{40,32},{48,40},{56,48},{64,56},{72,6... | collective-permute-start | bytes 393224 | tf_op jit(solution)/shard_map/ppermute | solution.py:29
  306.2 3.0 collective-permute-done.3
  309.3 0.6 divide_add_fusion
  309.9 1.3 log_multiply_fusion
  311.3 4.6 %all-to-all-start = ((f32[1,256,256]{2,0,1:T(1,128)}), f32[1,256,256]{2,0,1:T(1,128)S(1)}, u32[]{:S(2)}, u32[]{:S(2)}) async-start(f32[1,256,256]{2,0,1:T(1,128)} %get-tuple-element.244), calls=%async_computation | async-start | bytes 524288 | tf_op jit(solution)/shard_map/all_to_all | solution.py:143
  316.0 0.6 multiply_reduce_fusion.16
  317.3 5.8 %all-to-all-done = f32[1,256,256]{2,0,1:T(1,128)S(1)} async-done(((f32[1,256,256]{2,0,1:T(1,128)}), f32[1,256,256]{2,0,1:T(1,128)S(1)}, u32[]{:S(2)}, u32[]{:S(2)}) %all-to-all-start) | async-done | bytes 262176 | tf_op jit(solution)/shard_map/all_to_all | solution.py:143
  325.6 1.0 stack.9
  326.6 3.5 %all-to-all-start.1 = ((f32[8,3,32,256]{3,2,1,0:T(8,128)}), f32[8,3,32,256]{3,2,1,0:T(8,128)S(1)}, u32[]{:S(2)}, u32[]{:S(2)}) async-start(f32[8,3,32,256]{3,2,1,0:T(8,128)} %stack.9), calls=%async_computation.1 | async-start | bytes 1572864 | tf_op jit(solution)/shard_map/all_to_all | solution.py:146
  330.3 9.2 %all-to-all-done.1 = f32[8,3,32,256]{3,2,1,0:T(8,128)S(1)} async-done(((f32[8,3,32,256]{3,2,1,0:T(8,128)}), f32[8,3,32,256]{3,2,1,0:T(8,128)S(1)}, u32[]{:S(2)}, u32[]{:S(2)}) %all-to-all-start.1) | async-done | bytes 786464 | tf_op jit(solution)/shard_map/all_to_all | solution.py:146
  340.3 0.8 copy.107
  341.2 0.9 copy.106
  (155 shorter events, 22.8 us)
Async XLA Ops:
  2.1 10.0 %copy-start.2 = (f32[1,2,128,128]{3,2,1,0:T(8,128)S(1)}, f32[1,2,128,128]{3,2,1,0:T(8,128)}, u32[]{:S(2)}) copy-start(f32[1,2,128,128]{3,2,1,0:T(8,128)} %param.18) | copy-start | bytes 393220
  2.1 12.0 %collective-permute-start = (f32[2,64,256]{2,0,1:T(2,128)S(1)}, f32[2,64,256]{2,0,1:T(2,128)S(1)}, u32[]{:S(2)}, u32[]{:S(2)}) collective-permute-start(f32[2,64,256]{2,0,1:T(2,128)S(1)} %get-tuple-element.256), channel_id=1, source_target_pairs={{0,8},{8,16},{16,24},{24,32},{32,40},{40,48},{48,56},{56,64},{64,7... | collective-permute-start | bytes 393224 | tf_op jit(solution)/shard_map/ppermute | solution.py:20
  4.2 11.6 %collective-permute-start.1 = (f32[2,64,256]{2,0,1:T(2,128)S(1)}, f32[2,64,256]{2,0,1:T(2,128)S(1)}, u32[]{:S(2)}, u32[]{:S(2)}) collective-permute-start(f32[2,64,256]{2,0,1:T(2,128)S(1)} %get-tuple-element.257), channel_id=1, source_target_pairs={{8,0},{16,8},{24,16},{32,24},{40,32},{48,40},{56,48},{64,56},{72,6... | collective-permute-start | bytes 393224 | tf_op jit(solution)/shard_map/ppermute | solution.py:21
  12.1 0.7 copy-start.4
  12.7 0.7 copy-start.5
  41.6 1.2 copy-start
  285.6 20.1 %collective-permute-start.4 = (f32[64,256]{1,0:T(8,128)S(1)}, f32[64,256]{1,0:T(8,128)S(1)}, u32[]{:S(2)}, u32[]{:S(2)}) collective-permute-start(f32[64,256]{1,0:T(8,128)S(1)} %get-tuple-element.259), channel_id=1, source_target_pairs={{0,8},{8,16},{16,24},{24,32},{32,40},{40,48},{48,56},{56,64},{64,7... | collective-permute-start | bytes 196616 | tf_op jit(solution)/shard_map/ppermute | solution.py:29
  287.7 17.9 %collective-permute-start.5 = (f32[64,256]{1,0:T(8,128)S(1)}, f32[64,256]{1,0:T(8,128)S(1)}, u32[]{:S(2)}, u32[]{:S(2)}) collective-permute-start(f32[64,256]{1,0:T(8,128)S(1)} %get-tuple-element.258), channel_id=1, source_target_pairs={{8,0},{16,8},{24,16},{32,24},{40,32},{48,40},{56,48},{64,56},{72,6... | collective-permute-start | bytes 196616 | tf_op jit(solution)/shard_map/ppermute | solution.py:29
  295.6 10.5 %collective-permute-start.2 = (f32[2,64,256]{2,0,1:T(2,128)S(1)}, f32[2,64,256]{2,0,1:T(2,128)S(1)}, u32[]{:S(2)}, u32[]{:S(2)}) collective-permute-start(f32[2,64,256]{2,0,1:T(2,128)S(1)} %get-tuple-element.255), channel_id=1, source_target_pairs={{0,8},{8,16},{16,24},{24,32},{32,40},{40,48},{48,56},{56,64},{64,7... | collective-permute-start | bytes 393224 | tf_op jit(solution)/shard_map/ppermute | solution.py:29
  297.5 11.7 %collective-permute-start.3 = (f32[2,64,256]{2,0,1:T(2,128)S(1)}, f32[2,64,256]{2,0,1:T(2,128)S(1)}, u32[]{:S(2)}, u32[]{:S(2)}) collective-permute-start(f32[2,64,256]{2,0,1:T(2,128)S(1)} %get-tuple-element.254), channel_id=1, source_target_pairs={{8,0},{16,8},{24,16},{32,24},{40,32},{48,40},{56,48},{64,56},{72,6... | collective-permute-start | bytes 393224 | tf_op jit(solution)/shard_map/ppermute | solution.py:29
  305.7 3.6 %copy-start.1 = (f32[1,2,256,256]{3,2,1,0:T(8,128)S(1)}, f32[1,2,256,256]{3,2,1,0:T(8,128)}, u32[]{:S(2)}) copy-start(f32[1,2,256,256]{3,2,1,0:T(8,128)} %param.17) | copy-start | bytes 1572868
  311.3 4.6 %copy-start.3 = (f32[8,3]{0,1:T(4,128)S(1)}, f32[8,3]{0,1:T(4,128)}, u32[]{:S(2)}) copy-start(f32[8,3]{0,1:T(4,128)} %param.23) | copy-start | bytes 292
  311.3 11.8 %all-to-all-start = ((f32[1,256,256]{2,0,1:T(1,128)}), f32[1,256,256]{2,0,1:T(1,128)S(1)}, u32[]{:S(2)}, u32[]{:S(2)}) async-start(f32[1,256,256]{2,0,1:T(1,128)} %get-tuple-element.244), calls=%async_computation | async-start | bytes 524288 | tf_op jit(solution)/shard_map/all_to_all | solution.py:143
  326.6 13.0 %all-to-all-start.1 = ((f32[8,3,32,256]{3,2,1,0:T(8,128)}), f32[8,3,32,256]{3,2,1,0:T(8,128)S(1)}, u32[]{:S(2)}, u32[]{:S(2)}) async-start(f32[8,3,32,256]{3,2,1,0:T(8,128)} %stack.9), calls=%async_computation.1 | async-start | bytes 1572864 | tf_op jit(solution)/shard_map/all_to_all | solution.py:146
